TPU v7x, 256 devices: a whole 4x4x8 slice. The times are simulated.
256 devices in a mesh: leaf: 256 (over x, y, z, core).
Axes of the slice: x: 4, y: 4, z: 8, core: 2. Of those that a mesh axis runs over, the one named last changes fastest.
Arguments:
- right_side: bfloat16 [262144, 256], P('leaf'), may hold values from -6 to 6
- leaf_inv: bfloat16 [262144, 1024], P('leaf'), may hold values from -0.1875 to 0.1875
- right_basis: bfloat16 [4, 262144, 256], P(None, 'leaf'), may hold values from -0.0234375 to 0.0234375
- left_basis: bfloat16 [4, 262144, 256], P(None, 'leaf'), may hold values from -0.375 to 0.375
- reduced_first: float32 [512, 512], P('leaf'), may hold values from -0.25 to 0.25
- reduced_second: float32 [1024, 512], P('leaf'), may hold values from -0.25 to 0.25
- reduced_third: float32 [2048, 512], P('leaf'), may hold values from -0.25 to 0.25
- reduced_fourth: float32 [4096, 512], P('leaf'), may hold values from -0.25 to 0.25
Outputs:
- solution: float32 [262144, 256], P('leaf')
All inputs are finite; a program needn't handle non-finite values.
Results may differ from a plain program's by a relative error of at most 0.0003.
Values sent between devices are 32-bit elements; how exact they have to be, the bound alone decides.
No kernel may reach another device: no remote copies, remote signals or barrier semaphores. Data moves between devices by JAX's collectives and lax.ppermute only.
A program may use at most 64 MiB of HBM per device.

v0:
```python
import jax
import jax.numpy as jnp
from jax import lax
from jax.sharding import PartitionSpec as P

LEVELS = 4


def from_partner(block, axis, bit):
    count = lax.axis_size(axis)
    route = []
    for low in range(count):
        high = low | 1 << bit
        if high != low and high < count:
            route += [(low, high), (high, low)]
    return lax.ppermute(block, axis, route)


def bit_high(position, bitnum):
    return position >> bitnum & 1 == 1


def subtree_sum(partial_value, bit_count):
    totals = partial_value
    for bitnum in range(bit_count):
        totals = totals + from_partner(totals, "leaf", bitnum)
    return totals


def local(
    right_side,
    leaf_inv,
    right_basis,
    left_basis,
    reduced_first,
    reduced_second,
    reduced_third,
    reduced_fourth,
):
    devices_all = lax.axis_size("leaf")
    tree_depth = devices_all.bit_length() - 1
    position = lax.axis_index("leaf")
    reduced_all = (reduced_first, reduced_second, reduced_third, reduced_fourth)
    solution = jnp.dot(leaf_inv, right_side, preferred_element_type=jnp.float32)
    for level in range(LEVELS, 0, -1):
        child_bits = tree_depth - level
        right_rows = right_basis[level - 1].astype(jnp.float32)
        partial_value = lax.dot_general(
            right_rows,
            solution,
            (((0,), (0,)), ((), ())),
            precision=lax.Precision.HIGHEST,
            preferred_element_type=jnp.float32,
        )
        is_upper = bit_high(position, child_bits)
        own_sum = subtree_sum(partial_value, child_bits)
        other_sum = from_partner(own_sum, "leaf", child_bits)
        stacked = jnp.where(
            is_upper,
            jnp.concatenate([other_sum, own_sum], 0),
            jnp.concatenate([own_sum, other_sum], 0),
        )
        gathered = jnp.dot(
            reduced_all[level - 1],
            stacked,
            precision=lax.Precision.HIGHEST,
            preferred_element_type=jnp.float32,
        )
        for bitnum in range(child_bits):
            received = from_partner(gathered, "leaf", bitnum)
            is_high = bit_high(position, bitnum)
            gathered = jnp.where(
                is_high,
                jnp.concatenate([received, gathered], 0),
                jnp.concatenate([gathered, received], 0),
            )
        left_rows = left_basis[level - 1].astype(jnp.float32)
        solution = solution - jnp.dot(
            left_rows, gathered, precision=lax.Precision.HIGHEST, preferred_element_type=jnp.float32
        )
    return solution


def solution(mesh):
    return jax.shard_map(
        local,
        mesh=mesh,
        in_specs=(
            P("leaf", None),
            P("leaf", None),
            P(None, "leaf", None),
            P(None, "leaf", None),
            P("leaf", None),
            P("leaf", None),
            P("leaf", None),
            P("leaf", None),
        ),
        out_specs=P("leaf", None),
        check_vma=False,
    )
```

profile of v0, /device:TPU:1, one launch (start us, length us, event | category | flops | bytes accessed | tf_op | source)
XLA Modules:
  0.0 371.4 jit_solution(6559973113855525141)
XLA Ops:
  3.4 2.2 convolution_bitcast_fusion.7
  5.6 3.3 collective-permute-start
  10.2 7.5 %collective-permute-done.1 = f32[256,256]{1,0:T(8,128)S(1)} collective-permute-done((f32[256,256]{1,0:T(8,128)S(1)}, f32[256,256]{1,0:T(8,128)S(1)}, u32[]{:S(2)}, u32[]{:S(2)}) %collective-permute-start.1) | collective-permute-done | bytes 262176 | tf_op jit(solution)/shard_map/ppermute | solution.py:16
  19.4 12.8 %collective-permute-done.2 = f32[256,256]{1,0:T(8,128)S(1)} collective-permute-done((f32[256,256]{1,0:T(8,128)S(1)}, f32[256,256]{1,0:T(8,128)S(1)}, u32[]{:S(2)}, u32[]{:S(2)}) %collective-permute-start.2) | collective-permute-done | bytes 262176 | tf_op jit(solution)/shard_map/ppermute | solution.py:16
  32.3 5.1 %collective-permute-start.3 = (f32[256,256]{1,0:T(8,128)S(1)}, f32[256,256]{1,0:T(8,128)S(1)}, u32[]{:S(2)}, u32[]{:S(2)}) collective-permute-start(f32[256,256]{1,0:T(8,128)S(1)} %add.68), channel_id=1, source_target_pairs={{0,8},{8,0},{1,9},{9,1},{2,10},{10,2},{3,11},{11,3},{4,12},{12,4},... | collective-permute-start | bytes 786440 | tf_op jit(solution)/shard_map/ppermute | solution.py:16
  37.4 11.6 %collective-permute-done.3 = f32[256,256]{1,0:T(8,128)S(1)} collective-permute-done((f32[256,256]{1,0:T(8,128)S(1)}, f32[256,256]{1,0:T(8,128)S(1)}, u32[]{:S(2)}, u32[]{:S(2)}) %collective-permute-start.3) | collective-permute-done | bytes 262176 | tf_op jit(solution)/shard_map/ppermute | solution.py:16
  49.2 6.2 %collective-permute-done.4 = f32[256,256]{1,0:T(8,128)S(1)} collective-permute-done((f32[256,256]{1,0:T(8,128)S(1)}, f32[256,256]{1,0:T(8,128)S(1)}, u32[]{:S(2)}, u32[]{:S(2)}) %collective-permute-start.4) | collective-permute-done | bytes 262176 | tf_op jit(solution)/shard_map/ppermute | solution.py:16
  55.7 2.6 collective-permute-start.5
  59.2 2.8 collective-permute-done.6
  62.0 2.1 collective-permute-start.7
  64.0 2.0 collective-permute-done.7
  66.1 2.7 collective-permute-start.8
  68.8 5.2 %collective-permute-done.8 = f32[128,256]{1,0:T(8,128)S(1)} collective-permute-done((f32[128,256]{1,0:T(8,128)S(1)}, f32[128,256]{1,0:T(8,128)S(1)}, u32[]{:S(2)}, u32[]{:S(2)}) %collective-permute-start.8) | collective-permute-done | bytes 131104 | tf_op jit(solution)/shard_map/ppermute | solution.py:16
  74.0 2.0 fusion.3
  77.9 7.2 %collective-permute-start.9 = (f32[256,256]{1,0:T(8,128)S(1)}, f32[256,256]{1,0:T(8,128)S(1)}, u32[]{:S(2)}, u32[]{:S(2)}) collective-permute-start(f32[256,256]{1,0:T(8,128)S(1)} %convolution_bitcast_fusion.6), channel_id=1, source_target_pairs={{0,1},{1,0},{2,3},{3,2},{4,5},{5,4},{6,7},{7,6},{8,9},{9,8},{10,11... | collective-permute-start | bytes 786440 | tf_op jit(solution)/shard_map/ppermute | solution.py:16
  86.3 7.5 %collective-permute-done.10 = f32[256,256]{1,0:T(8,128)S(1)} collective-permute-done((f32[256,256]{1,0:T(8,128)S(1)}, f32[256,256]{1,0:T(8,128)S(1)}, u32[]{:S(2)}, u32[]{:S(2)}) %collective-permute-start.10) | collective-permute-done | bytes 262176 | tf_op jit(solution)/shard_map/ppermute | solution.py:16
  94.0 14.7 %collective-permute-done.11 = f32[256,256]{1,0:T(8,128)S(1)} collective-permute-done((f32[256,256]{1,0:T(8,128)S(1)}, f32[256,256]{1,0:T(8,128)S(1)}, u32[]{:S(2)}, u32[]{:S(2)}) %collective-permute-start.11) | collective-permute-done | bytes 262176 | tf_op jit(solution)/shard_map/ppermute | solution.py:16
  110.4 14.7 %collective-permute-done.12 = f32[256,256]{1,0:T(8,128)S(1)} collective-permute-done((f32[256,256]{1,0:T(8,128)S(1)}, f32[256,256]{1,0:T(8,128)S(1)}, u32[]{:S(2)}, u32[]{:S(2)}) %collective-permute-start.12) | collective-permute-done | bytes 262176 | tf_op jit(solution)/shard_map/ppermute | solution.py:16
  125.2 7.4 %collective-permute-done.13 = f32[256,256]{1,0:T(8,128)S(1)} collective-permute-done((f32[256,256]{1,0:T(8,128)S(1)}, f32[256,256]{1,0:T(8,128)S(1)}, u32[]{:S(2)}, u32[]{:S(2)}) %collective-permute-start.13) | collective-permute-done | bytes 262176 | tf_op jit(solution)/shard_map/ppermute | solution.py:16
  133.8 7.0 %collective-permute-done.14 = f32[256,256]{1,0:T(8,128)} collective-permute-done((f32[256,256]{1,0:T(8,128)S(1)}, f32[256,256]{1,0:T(8,128)}, u32[]{:S(2)}, u32[]{:S(2)}) %collective-permute-start.14) | collective-permute-done | bytes 262176 | tf_op jit(solution)/shard_map/ppermute | solution.py:16
  142.2 2.4 collective-permute-start.15
  145.5 2.6 collective-permute-done.16
  148.2 3.6 collective-permute-done.17
  151.8 2.1 collective-permute-start.18
  154.0 5.0 %collective-permute-done.18 = f32[64,256]{1,0:T(8,128)S(1)} collective-permute-done((f32[64,256]{1,0:T(8,128)S(1)}, f32[64,256]{1,0:T(8,128)S(1)}, u32[]{:S(2)}, u32[]{:S(2)}) %collective-permute-start.18) | collective-permute-done | bytes 65568 | tf_op jit(solution)/shard_map/ppermute | solution.py:16
  159.5 3.4 collective-permute-done.19
  164.6 2.2 convolution_bitcast_fusion.5
  166.8 5.6 %collective-permute-start.20 = (f32[256,256]{1,0:T(8,128)S(1)}, f32[256,256]{1,0:T(8,128)S(1)}, u32[]{:S(2)}, u32[]{:S(2)}) collective-permute-start(f32[256,256]{1,0:T(8,128)S(1)} %convolution_bitcast_fusion.5), channel_id=1, source_target_pairs={{0,1},{1,0},{2,3},{3,2},{4,5},{5,4},{6,7},{7,6},{8,9},{9,8},{10,11... | collective-permute-start | bytes 786440 | tf_op jit(solution)/shard_map/ppermute | solution.py:16
  173.7 7.5 %collective-permute-done.21 = f32[256,256]{1,0:T(8,128)S(1)} collective-permute-done((f32[256,256]{1,0:T(8,128)S(1)}, f32[256,256]{1,0:T(8,128)S(1)}, u32[]{:S(2)}, u32[]{:S(2)}) %collective-permute-start.21) | collective-permute-done | bytes 262176 | tf_op jit(solution)/shard_map/ppermute | solution.py:16
  181.7 14.3 %collective-permute-done.22 = f32[256,256]{1,0:T(8,128)S(1)} collective-permute-done((f32[256,256]{1,0:T(8,128)S(1)}, f32[256,256]{1,0:T(8,128)S(1)}, u32[]{:S(2)}, u32[]{:S(2)}) %collective-permute-start.22) | collective-permute-done | bytes 262176 | tf_op jit(solution)/shard_map/ppermute | solution.py:16
  196.8 14.2 %collective-permute-done.23 = f32[256,256]{1,0:T(8,128)S(1)} collective-permute-done((f32[256,256]{1,0:T(8,128)S(1)}, f32[256,256]{1,0:T(8,128)S(1)}, u32[]{:S(2)}, u32[]{:S(2)}) %collective-permute-start.23) | collective-permute-done | bytes 262176 | tf_op jit(solution)/shard_map/ppermute | solution.py:16
  211.8 6.3 %collective-permute-done.24 = f32[256,256]{1,0:T(8,128)S(1)} collective-permute-done((f32[256,256]{1,0:T(8,128)S(1)}, f32[256,256]{1,0:T(8,128)S(1)}, u32[]{:S(2)}, u32[]{:S(2)}) %collective-permute-start.24) | collective-permute-done | bytes 262176 | tf_op jit(solution)/shard_map/ppermute | solution.py:16
  218.2 3.0 collective-permute-start.25
  221.2 4.6 %collective-permute-done.25 = f32[256,256]{1,0:T(8,128)S(1)} collective-permute-done((f32[256,256]{1,0:T(8,128)S(1)}, f32[256,256]{1,0:T(8,128)S(1)}, u32[]{:S(2)}, u32[]{:S(2)}) %collective-permute-start.25) | collective-permute-done | bytes 262176 | tf_op jit(solution)/shard_map/ppermute | solution.py:16
  227.5 3.8 %collective-permute-done.26 = f32[256,256]{1,0:T(8,128)S(1)} collective-permute-done((f32[256,256]{1,0:T(8,128)S(1)}, f32[256,256]{1,0:T(8,128)S(1)}, u32[]{:S(2)}, u32[]{:S(2)}) %collective-permute-start.26) | collective-permute-done | bytes 262176 | tf_op jit(solution)/shard_map/ppermute | solution.py:16
  231.6 3.7 %collective-permute-start.27 = (f32[4,256]{1,0:T(4,128)S(1)}, f32[4,256]{1,0:T(4,128)S(1)}, u32[]{:S(2)}, u32[]{:S(2)}) collective-permute-start(f32[4,256]{1,0:T(4,128)S(1)} %convolution_bitcast_fusion.10), channel_id=1, source_target_pairs={{0,1},{1,0},{2,3},{3,2},{4,5},{5,4},{6,7},{7,6},{8,9},{9,8},{10,11... | collective-permute-start | bytes 12296 | tf_op jit(solution)/shard_map/ppermute | solution.py:16
  236.2 2.5 collective-permute-done.28
  238.7 3.5 collective-permute-start.29
  243.3 2.4 collective-permute-start.30
  245.7 4.2 %collective-permute-done.30 = f32[32,256]{1,0:T(8,128)S(1)} collective-permute-done((f32[32,256]{1,0:T(8,128)S(1)}, f32[32,256]{1,0:T(8,128)S(1)}, u32[]{:S(2)}, u32[]{:S(2)}) %collective-permute-start.30) | collective-permute-done | bytes 32800 | tf_op jit(solution)/shard_map/ppermute | solution.py:16
  250.9 2.3 collective-permute-done.31
  253.2 2.9 collective-permute-start.32
  256.1 3.1 collective-permute-done.32
  262.6 5.6 %collective-permute-start.33 = (f32[256,256]{1,0:T(8,128)S(1)}, f32[256,256]{1,0:T(8,128)S(1)}, u32[]{:S(2)}, u32[]{:S(2)}) collective-permute-start(f32[256,256]{1,0:T(8,128)S(1)} %convolution_bitcast_fusion.4), channel_id=1, source_target_pairs={{0,1},{1,0},{2,3},{3,2},{4,5},{5,4},{6,7},{7,6},{8,9},{9,8},{10,11... | collective-permute-start | bytes 786440 | tf_op jit(solution)/shard_map/ppermute | solution.py:16
  271.1 6.1 %collective-permute-done.34 = f32[256,256]{1,0:T(8,128)S(1)} collective-permute-done((f32[256,256]{1,0:T(8,128)S(1)}, f32[256,256]{1,0:T(8,128)S(1)}, u32[]{:S(2)}, u32[]{:S(2)}) %collective-permute-start.34) | collective-permute-done | bytes 262176 | tf_op jit(solution)/shard_map/ppermute | solution.py:16
  277.3 3.0 collective-permute-start.35
  280.3 11.5 %collective-permute-done.35 = f32[256,256]{1,0:T(8,128)S(1)} collective-permute-done((f32[256,256]{1,0:T(8,128)S(1)}, f32[256,256]{1,0:T(8,128)S(1)}, u32[]{:S(2)}, u32[]{:S(2)}) %collective-permute-start.35) | collective-permute-done | bytes 262176 | tf_op jit(solution)/shard_map/ppermute | solution.py:16
  291.8 2.1 collective-permute-start.36
  293.9 15.1 %collective-permute-done.36 = f32[256,256]{1,0:T(8,128)S(1)} collective-permute-done((f32[256,256]{1,0:T(8,128)S(1)}, f32[256,256]{1,0:T(8,128)S(1)}, u32[]{:S(2)}, u32[]{:S(2)}) %collective-permute-start.36) | collective-permute-done | bytes 262176 | tf_op jit(solution)/shard_map/ppermute | solution.py:16
  309.8 6.6 %collective-permute-done.37 = f32[256,256]{1,0:T(8,128)S(1)} collective-permute-done((f32[256,256]{1,0:T(8,128)S(1)}, f32[256,256]{1,0:T(8,128)S(1)}, u32[]{:S(2)}, u32[]{:S(2)}) %collective-permute-start.37) | collective-permute-done | bytes 262176 | tf_op jit(solution)/shard_map/ppermute | solution.py:16
  316.5 3.3 collective-permute-start.38
  319.8 5.3 %collective-permute-done.38 = f32[256,256]{1,0:T(8,128)S(1)} collective-permute-done((f32[256,256]{1,0:T(8,128)S(1)}, f32[256,256]{1,0:T(8,128)S(1)}, u32[]{:S(2)}, u32[]{:S(2)}) %collective-permute-start.38) | collective-permute-done | bytes 262176 | tf_op jit(solution)/shard_map/ppermute | solution.py:16
  326.3 4.8 %collective-permute-done.39 = f32[256,256]{1,0:T(8,128)S(1)} collective-permute-done((f32[256,256]{1,0:T(8,128)S(1)}, f32[256,256]{1,0:T(8,128)S(1)}, u32[]{:S(2)}, u32[]{:S(2)}) %collective-permute-start.39) | collective-permute-done | bytes 262176 | tf_op jit(solution)/shard_map/ppermute | solution.py:16
  331.2 2.8 collective-permute-start.40
  334.0 4.2 %collective-permute-done.40 = f32[256,256]{1,0:T(8,128)} collective-permute-done((f32[256,256]{1,0:T(8,128)S(1)}, f32[256,256]{1,0:T(8,128)}, u32[]{:S(2)}, u32[]{:S(2)}) %collective-permute-start.40) | collective-permute-done | bytes 262176 | tf_op jit(solution)/shard_map/ppermute | solution.py:16
  339.5 4.0 %collective-permute-start.41 = (f32[2,256]{1,0:T(2,128)S(1)}, f32[2,256]{1,0:T(2,128)S(1)}, u32[]{:S(2)}, u32[]{:S(2)}) collective-permute-start(f32[2,256]{1,0:T(2,128)S(1)} %convolution_bitcast_fusion.11), channel_id=1, source_target_pairs={{0,1},{1,0},{2,3},{3,2},{4,5},{5,4},{6,7},{7,6},{8,9},{9,8},{10,11... | collective-permute-start | bytes 6152 | tf_op jit(solution)/shard_map/ppermute | solution.py:16
  344.3 2.4 collective-permute-done.42
  346.8 2.7 collective-permute-start.43
  350.6 3.0 collective-permute-start.44
  353.5 3.5 collective-permute-done.44
  357.9 2.3 collective-permute-done.45
  360.1 2.8 collective-permute-start.46
  366.1 2.7 collective-permute-done.47
  368.8 2.6 fusion
  (101 shorter events, 42.8 us)
Async XLA Ops:
  0.0 1.6 copy-start
  3.4 28.9 %copy-start.3 = (f32[1024,256]{1,0:T(8,128)}, f32[1024,256]{1,0:T(8,128)S(1)}, u32[]{:S(2)}) copy-start(f32[1024,256]{1,0:T(8,128)S(1)} %fusion.76) | copy-start | bytes 3145732
  3.4 52.0 %copy-start.4 = (f32[16,512]{1,0:T(8,128)S(1)}, f32[16,512]{1,0:T(8,128)}, u32[]{:S(2)}) copy-start(f32[16,512]{1,0:T(8,128)} %param.15) | copy-start | bytes 98308
  5.6 4.5 %collective-permute-start = (f32[256,256]{1,0:T(8,128)S(1)}, f32[256,256]{1,0:T(8,128)S(1)}, u32[]{:S(2)}, u32[]{:S(2)}) collective-permute-start(f32[256,256]{1,0:T(8,128)S(1)} %convolution_bitcast_fusion.7), channel_id=1, source_target_pairs={{0,1},{1,0},{2,3},{3,2},{4,5},{5,4},{6,7},{7,6},{8,9},{9,8},{10,11... | collective-permute-start | bytes 786440 | tf_op jit(solution)/shard_map/ppermute | solution.py:16
  10.1 7.6 %collective-permute-start.1 = (f32[256,256]{1,0:T(8,128)S(1)}, f32[256,256]{1,0:T(8,128)S(1)}, u32[]{:S(2)}, u32[]{:S(2)}) collective-permute-start(f32[256,256]{1,0:T(8,128)S(1)} %add.66), channel_id=1, source_target_pairs={{0,2},{2,0},{1,3},{3,1},{4,6},{6,4},{5,7},{7,5},{8,10},{10,8},{9,1... | collective-permute-start | bytes 786440 | tf_op jit(solution)/shard_map/ppermute | solution.py:16
  17.7 14.6 %collective-permute-start.2 = (f32[256,256]{1,0:T(8,128)S(1)}, f32[256,256]{1,0:T(8,128)S(1)}, u32[]{:S(2)}, u32[]{:S(2)}) collective-permute-start(f32[256,256]{1,0:T(8,128)S(1)} %add.67), channel_id=1, source_target_pairs={{0,4},{4,0},{1,5},{5,1},{2,6},{6,2},{3,7},{7,3},{8,12},{12,8},{9,1... | collective-permute-start | bytes 786440 | tf_op jit(solution)/shard_map/ppermute | solution.py:16
  32.3 16.7 %collective-permute-start.3 = (f32[256,256]{1,0:T(8,128)S(1)}, f32[256,256]{1,0:T(8,128)S(1)}, u32[]{:S(2)}, u32[]{:S(2)}) collective-permute-start(f32[256,256]{1,0:T(8,128)S(1)} %add.68), channel_id=1, source_target_pairs={{0,8},{8,0},{1,9},{9,1},{2,10},{10,2},{3,11},{11,3},{4,12},{12,4},... | collective-permute-start | bytes 786440 | tf_op jit(solution)/shard_map/ppermute | solution.py:16
  49.1 6.3 %collective-permute-start.4 = (f32[256,256]{1,0:T(8,128)S(1)}, f32[256,256]{1,0:T(8,128)S(1)}, u32[]{:S(2)}, u32[]{:S(2)}) collective-permute-start(f32[256,256]{1,0:T(8,128)S(1)} %add.69), channel_id=1, source_target_pairs={{0,16},{16,0},{1,17},{17,1},{2,18},{18,2},{3,19},{19,3},{4,20},{20... | collective-permute-start | bytes 786440 | tf_op jit(solution)/shard_map/ppermute | solution.py:16
  55.7 3.5 collective-permute-start.5
  59.2 2.8 collective-permute-start.6
  62.0 4.1 %collective-permute-start.7 = (f32[64,256]{1,0:T(8,128)S(1)}, f32[64,256]{1,0:T(8,128)S(1)}, u32[]{:S(2)}, u32[]{:S(2)}) collective-permute-start(f32[64,256]{1,0:T(8,128)S(1)} %maximum_select_fusion.20), channel_id=1, source_target_pairs={{0,4},{4,0},{1,5},{5,1},{2,6},{6,2},{3,7},{7,3},{8,12},{12,8},{9,1... | collective-permute-start | bytes 196616 | tf_op jit(solution)/shard_map/ppermute | solution.py:16
  66.1 7.9 %collective-permute-start.8 = (f32[128,256]{1,0:T(8,128)S(1)}, f32[128,256]{1,0:T(8,128)S(1)}, u32[]{:S(2)}, u32[]{:S(2)}) collective-permute-start(f32[128,256]{1,0:T(8,128)S(1)} %maximum_select_fusion.16), channel_id=1, source_target_pairs={{0,8},{8,0},{1,9},{9,1},{2,10},{10,2},{3,11},{11,3},{4,12},{12,4},... | collective-permute-start | bytes 393224 | tf_op jit(solution)/shard_map/ppermute | solution.py:16
  77.8 63.0 %copy-start.5 = (f32[8,512]{1,0:T(8,128)S(1)}, f32[8,512]{1,0:T(8,128)}, u32[]{:S(2)}) copy-start(f32[8,512]{1,0:T(8,128)} %param.14) | copy-start | bytes 49156
  77.9 8.4 %collective-permute-start.9 = (f32[256,256]{1,0:T(8,128)S(1)}, f32[256,256]{1,0:T(8,128)S(1)}, u32[]{:S(2)}, u32[]{:S(2)}) collective-permute-start(f32[256,256]{1,0:T(8,128)S(1)} %convolution_bitcast_fusion.6), channel_id=1, source_target_pairs={{0,1},{1,0},{2,3},{3,2},{4,5},{5,4},{6,7},{7,6},{8,9},{9,8},{10,11... | collective-permute-start | bytes 786440 | tf_op jit(solution)/shard_map/ppermute | solution.py:16
  86.2 7.6 %collective-permute-start.10 = (f32[256,256]{1,0:T(8,128)S(1)}, f32[256,256]{1,0:T(8,128)S(1)}, u32[]{:S(2)}, u32[]{:S(2)}) collective-permute-start(f32[256,256]{1,0:T(8,128)S(1)} %add.70), channel_id=1, source_target_pairs={{0,2},{2,0},{1,3},{3,1},{4,6},{6,4},{5,7},{7,5},{8,10},{10,8},{9,1... | collective-permute-start | bytes 786440 | tf_op jit(solution)/shard_map/ppermute | solution.py:16
  93.9 14.8 %collective-permute-start.11 = (f32[256,256]{1,0:T(8,128)S(1)}, f32[256,256]{1,0:T(8,128)S(1)}, u32[]{:S(2)}, u32[]{:S(2)}) collective-permute-start(f32[256,256]{1,0:T(8,128)S(1)} %add.71), channel_id=1, source_target_pairs={{0,4},{4,0},{1,5},{5,1},{2,6},{6,2},{3,7},{7,3},{8,12},{12,8},{9,1... | collective-permute-start | bytes 786440 | tf_op jit(solution)/shard_map/ppermute | solution.py:16
  108.7 16.4 %collective-permute-start.12 = (f32[256,256]{1,0:T(8,128)S(1)}, f32[256,256]{1,0:T(8,128)S(1)}, u32[]{:S(2)}, u32[]{:S(2)}) collective-permute-start(f32[256,256]{1,0:T(8,128)S(1)} %add.72), channel_id=1, source_target_pairs={{0,8},{8,0},{1,9},{9,1},{2,10},{10,2},{3,11},{11,3},{4,12},{12,4},... | collective-permute-start | bytes 786440 | tf_op jit(solution)/shard_map/ppermute | solution.py:16
  125.1 7.5 %collective-permute-start.13 = (f32[256,256]{1,0:T(8,128)S(1)}, f32[256,256]{1,0:T(8,128)S(1)}, u32[]{:S(2)}, u32[]{:S(2)}) collective-permute-start(f32[256,256]{1,0:T(8,128)S(1)} %add.73), channel_id=1, source_target_pairs={{0,16},{16,0},{1,17},{17,1},{2,18},{18,2},{3,19},{19,3},{4,20},{20... | collective-permute-start | bytes 786440 | tf_op jit(solution)/shard_map/ppermute | solution.py:16
  132.6 8.2 %collective-permute-start.14 = (f32[256,256]{1,0:T(8,128)S(1)}, f32[256,256]{1,0:T(8,128)}, u32[]{:S(2)}, u32[]{:S(2)}) collective-permute-start(f32[256,256]{1,0:T(8,128)S(1)} %add.74), channel_id=1, source_target_pairs={{0,32},{32,0},{1,33},{33,1},{2,34},{34,2},{3,35},{35,3},{4,36},{36... | collective-permute-start | bytes 786440 | tf_op jit(solution)/shard_map/ppermute | solution.py:16
  142.2 3.3 collective-permute-start.15
  145.5 2.6 collective-permute-start.16
  148.1 3.7 %collective-permute-start.17 = (f32[32,256]{1,0:T(8,128)S(1)}, f32[32,256]{1,0:T(8,128)S(1)}, u32[]{:S(2)}, u32[]{:S(2)}) collective-permute-start(f32[32,256]{1,0:T(8,128)S(1)} %maximum_select_fusion.25), channel_id=1, source_target_pairs={{0,4},{4,0},{1,5},{5,1},{2,6},{6,2},{3,7},{7,3},{8,12},{12,8},{9,1... | collective-permute-start | bytes 98312 | tf_op jit(solution)/shard_map/ppermute | solution.py:16
  151.8 7.1 %collective-permute-start.18 = (f32[64,256]{1,0:T(8,128)S(1)}, f32[64,256]{1,0:T(8,128)S(1)}, u32[]{:S(2)}, u32[]{:S(2)}) collective-permute-start(f32[64,256]{1,0:T(8,128)S(1)} %maximum_select_fusion.21), channel_id=1, source_target_pairs={{0,8},{8,0},{1,9},{9,1},{2,10},{10,2},{3,11},{11,3},{4,12},{12,4},... | collective-permute-start | bytes 196616 | tf_op jit(solution)/shard_map/ppermute | solution.py:16
  158.9 4.0 %collective-permute-start.19 = (f32[128,256]{1,0:T(8,128)S(1)}, f32[128,256]{1,0:T(8,128)S(1)}, u32[]{:S(2)}, u32[]{:S(2)}) collective-permute-start(f32[128,256]{1,0:T(8,128)S(1)} %maximum_select_fusion.17), channel_id=1, source_target_pairs={{0,16},{16,0},{1,17},{17,1},{2,18},{18,2},{3,19},{19,3},{4,20},{20... | collective-permute-start | bytes 393224 | tf_op jit(solution)/shard_map/ppermute | solution.py:16
  164.6 31.5 %copy-start.1 = (f32[1024,256]{1,0:T(8,128)}, f32[1024,256]{1,0:T(8,128)S(1)}, u32[]{:S(2)}) copy-start(f32[1024,256]{1,0:T(8,128)S(1)} %fusion.2) | copy-start | bytes 3145732
  166.8 6.7 %collective-permute-start.20 = (f32[256,256]{1,0:T(8,128)S(1)}, f32[256,256]{1,0:T(8,128)S(1)}, u32[]{:S(2)}, u32[]{:S(2)}) collective-permute-start(f32[256,256]{1,0:T(8,128)S(1)} %convolution_bitcast_fusion.5), channel_id=1, source_target_pairs={{0,1},{1,0},{2,3},{3,2},{4,5},{5,4},{6,7},{7,6},{8,9},{9,8},{10,11... | collective-permute-start | bytes 786440 | tf_op jit(solution)/shard_map/ppermute | solution.py:16
  173.6 57.7 %copy-start.6 = (f32[4,512]{1,0:T(4,128)S(1)}, f32[4,512]{1,0:T(4,128)}, u32[]{:S(2)}) copy-start(f32[4,512]{1,0:T(4,128)} %param.13) | copy-start | bytes 24580
  173.6 7.6 %collective-permute-start.21 = (f32[256,256]{1,0:T(8,128)S(1)}, f32[256,256]{1,0:T(8,128)S(1)}, u32[]{:S(2)}, u32[]{:S(2)}) collective-permute-start(f32[256,256]{1,0:T(8,128)S(1)} %add.75), channel_id=1, source_target_pairs={{0,2},{2,0},{1,3},{3,1},{4,6},{6,4},{5,7},{7,5},{8,10},{10,8},{9,1... | collective-permute-start | bytes 786440 | tf_op jit(solution)/shard_map/ppermute | solution.py:16
  181.2 14.8 %collective-permute-start.22 = (f32[256,256]{1,0:T(8,128)S(1)}, f32[256,256]{1,0:T(8,128)S(1)}, u32[]{:S(2)}, u32[]{:S(2)}) collective-permute-start(f32[256,256]{1,0:T(8,128)S(1)} %add.76), channel_id=1, source_target_pairs={{0,4},{4,0},{1,5},{5,1},{2,6},{6,2},{3,7},{7,3},{8,12},{12,8},{9,1... | collective-permute-start | bytes 786440 | tf_op jit(solution)/shard_map/ppermute | solution.py:16
  196.1 15.0 %collective-permute-start.23 = (f32[256,256]{1,0:T(8,128)S(1)}, f32[256,256]{1,0:T(8,128)S(1)}, u32[]{:S(2)}, u32[]{:S(2)}) collective-permute-start(f32[256,256]{1,0:T(8,128)S(1)} %add.77), channel_id=1, source_target_pairs={{0,8},{8,0},{1,9},{9,1},{2,10},{10,2},{3,11},{11,3},{4,12},{12,4},... | collective-permute-start | bytes 786440 | tf_op jit(solution)/shard_map/ppermute | solution.py:16
  211.1 7.0 %collective-permute-start.24 = (f32[256,256]{1,0:T(8,128)S(1)}, f32[256,256]{1,0:T(8,128)S(1)}, u32[]{:S(2)}, u32[]{:S(2)}) collective-permute-start(f32[256,256]{1,0:T(8,128)S(1)} %add.78), channel_id=1, source_target_pairs={{0,16},{16,0},{1,17},{17,1},{2,18},{18,2},{3,19},{19,3},{4,20},{20... | collective-permute-start | bytes 786440 | tf_op jit(solution)/shard_map/ppermute | solution.py:16
  218.2 7.7 %collective-permute-start.25 = (f32[256,256]{1,0:T(8,128)S(1)}, f32[256,256]{1,0:T(8,128)S(1)}, u32[]{:S(2)}, u32[]{:S(2)}) collective-permute-start(f32[256,256]{1,0:T(8,128)S(1)} %add.79), channel_id=1, source_target_pairs={{0,32},{32,0},{1,33},{33,1},{2,34},{34,2},{3,35},{35,3},{4,36},{36... | collective-permute-start | bytes 786440 | tf_op jit(solution)/shard_map/ppermute | solution.py:16
  225.9 5.4 %collective-permute-start.26 = (f32[256,256]{1,0:T(8,128)S(1)}, f32[256,256]{1,0:T(8,128)S(1)}, u32[]{:S(2)}, u32[]{:S(2)}) collective-permute-start(f32[256,256]{1,0:T(8,128)S(1)} %add.80), channel_id=1, source_target_pairs={{0,64},{64,0},{1,65},{65,1},{2,66},{66,2},{3,67},{67,3},{4,68},{68... | collective-permute-start | bytes 786440 | tf_op jit(solution)/shard_map/ppermute | solution.py:16
  227.5 31.6 %copy-start.2 = (f32[1024,256]{1,0:T(8,128)S(1)}, f32[1024,256]{1,0:T(8,128)}, u32[]{:S(2)}) copy-start(f32[1024,256]{1,0:T(8,128)} %copy-done.1) | copy-start | bytes 3145732
  231.6 4.6 %collective-permute-start.27 = (f32[4,256]{1,0:T(4,128)S(1)}, f32[4,256]{1,0:T(4,128)S(1)}, u32[]{:S(2)}, u32[]{:S(2)}) collective-permute-start(f32[4,256]{1,0:T(4,128)S(1)} %convolution_bitcast_fusion.10), channel_id=1, source_target_pairs={{0,1},{1,0},{2,3},{3,2},{4,5},{5,4},{6,7},{7,6},{8,9},{9,8},{10,11... | collective-permute-start | bytes 12296 | tf_op jit(solution)/shard_map/ppermute | solution.py:16
  236.2 2.5 collective-permute-start.28
  238.7 4.6 %collective-permute-start.29 = (f32[16,256]{1,0:T(8,128)S(1)}, f32[16,256]{1,0:T(8,128)S(1)}, u32[]{:S(2)}, u32[]{:S(2)}) collective-permute-start(f32[16,256]{1,0:T(8,128)S(1)} %maximum_select_fusion.29), channel_id=1, source_target_pairs={{0,4},{4,0},{1,5},{5,1},{2,6},{6,2},{3,7},{7,3},{8,12},{12,8},{9,1... | collective-permute-start | bytes 49160 | tf_op jit(solution)/shard_map/ppermute | solution.py:16
  243.3 6.7 %collective-permute-start.30 = (f32[32,256]{1,0:T(8,128)S(1)}, f32[32,256]{1,0:T(8,128)S(1)}, u32[]{:S(2)}, u32[]{:S(2)}) collective-permute-start(f32[32,256]{1,0:T(8,128)S(1)} %maximum_select_fusion.26), channel_id=1, source_target_pairs={{0,8},{8,0},{1,9},{9,1},{2,10},{10,2},{3,11},{11,3},{4,12},{12,4},... | collective-permute-start | bytes 98312 | tf_op jit(solution)/shard_map/ppermute | solution.py:16
  250.0 3.2 collective-permute-start.31
  253.2 5.9 %collective-permute-start.32 = (f32[128,256]{1,0:T(8,128)S(1)}, f32[128,256]{1,0:T(8,128)S(1)}, u32[]{:S(2)}, u32[]{:S(2)}) collective-permute-start(f32[128,256]{1,0:T(8,128)S(1)} %maximum_select_fusion.18), channel_id=1, source_target_pairs={{0,32},{32,0},{1,33},{33,1},{2,34},{34,2},{3,35},{35,3},{4,36},{36... | collective-permute-start | bytes 393224 | tf_op jit(solution)/shard_map/ppermute | solution.py:16
  262.6 6.8 %collective-permute-start.33 = (f32[256,256]{1,0:T(8,128)S(1)}, f32[256,256]{1,0:T(8,128)S(1)}, u32[]{:S(2)}, u32[]{:S(2)}) collective-permute-start(f32[256,256]{1,0:T(8,128)S(1)} %convolution_bitcast_fusion.4), channel_id=1, source_target_pairs={{0,1},{1,0},{2,3},{3,2},{4,5},{5,4},{6,7},{7,6},{8,9},{9,8},{10,11... | collective-permute-start | bytes 786440 | tf_op jit(solution)/shard_map/ppermute | solution.py:16
  269.5 7.8 %collective-permute-start.34 = (f32[256,256]{1,0:T(8,128)S(1)}, f32[256,256]{1,0:T(8,128)S(1)}, u32[]{:S(2)}, u32[]{:S(2)}) collective-permute-start(f32[256,256]{1,0:T(8,128)S(1)} %add.81), channel_id=1, source_target_pairs={{0,2},{2,0},{1,3},{3,1},{4,6},{6,4},{5,7},{7,5},{8,10},{10,8},{9,1... | collective-permute-start | bytes 786440 | tf_op jit(solution)/shard_map/ppermute | solution.py:16
  277.3 60.9 %copy-start.7 = (f32[2,512]{1,0:T(2,128)S(1)}, f32[2,512]{1,0:T(2,128)}, u32[]{:S(2)}) copy-start(f32[2,512]{1,0:T(2,128)} %param.12) | copy-start | bytes 12292
  277.3 14.5 %collective-permute-start.35 = (f32[256,256]{1,0:T(8,128)S(1)}, f32[256,256]{1,0:T(8,128)S(1)}, u32[]{:S(2)}, u32[]{:S(2)}) collective-permute-start(f32[256,256]{1,0:T(8,128)S(1)} %add.82), channel_id=1, source_target_pairs={{0,4},{4,0},{1,5},{5,1},{2,6},{6,2},{3,7},{7,3},{8,12},{12,8},{9,1... | collective-permute-start | bytes 786440 | tf_op jit(solution)/shard_map/ppermute | solution.py:16
  291.8 17.2 %collective-permute-start.36 = (f32[256,256]{1,0:T(8,128)S(1)}, f32[256,256]{1,0:T(8,128)S(1)}, u32[]{:S(2)}, u32[]{:S(2)}) collective-permute-start(f32[256,256]{1,0:T(8,128)S(1)} %add.83), channel_id=1, source_target_pairs={{0,8},{8,0},{1,9},{9,1},{2,10},{10,2},{3,11},{11,3},{4,12},{12,4},... | collective-permute-start | bytes 786440 | tf_op jit(solution)/shard_map/ppermute | solution.py:16
  309.0 7.5 %collective-permute-start.37 = (f32[256,256]{1,0:T(8,128)S(1)}, f32[256,256]{1,0:T(8,128)S(1)}, u32[]{:S(2)}, u32[]{:S(2)}) collective-permute-start(f32[256,256]{1,0:T(8,128)S(1)} %add.84), channel_id=1, source_target_pairs={{0,16},{16,0},{1,17},{17,1},{2,18},{18,2},{3,19},{19,3},{4,20},{20... | collective-permute-start | bytes 786440 | tf_op jit(solution)/shard_map/ppermute | solution.py:16
  316.5 8.6 %collective-permute-start.38 = (f32[256,256]{1,0:T(8,128)S(1)}, f32[256,256]{1,0:T(8,128)S(1)}, u32[]{:S(2)}, u32[]{:S(2)}) collective-permute-start(f32[256,256]{1,0:T(8,128)S(1)} %add.85), channel_id=1, source_target_pairs={{0,32},{32,0},{1,33},{33,1},{2,34},{34,2},{3,35},{35,3},{4,36},{36... | collective-permute-start | bytes 786440 | tf_op jit(solution)/shard_map/ppermute | solution.py:16
  325.2 6.0 %collective-permute-start.39 = (f32[256,256]{1,0:T(8,128)S(1)}, f32[256,256]{1,0:T(8,128)S(1)}, u32[]{:S(2)}, u32[]{:S(2)}) collective-permute-start(f32[256,256]{1,0:T(8,128)S(1)} %add.86), channel_id=1, source_target_pairs={{0,64},{64,0},{1,65},{65,1},{2,66},{66,2},{3,67},{67,3},{4,68},{68... | collective-permute-start | bytes 786440 | tf_op jit(solution)/shard_map/ppermute | solution.py:16
  331.2 7.0 %collective-permute-start.40 = (f32[256,256]{1,0:T(8,128)S(1)}, f32[256,256]{1,0:T(8,128)}, u32[]{:S(2)}, u32[]{:S(2)}) collective-permute-start(f32[256,256]{1,0:T(8,128)S(1)} %add.87), channel_id=1, source_target_pairs={{0,128},{128,0},{1,129},{129,1},{2,130},{130,2},{3,131},{131,3},{4... | collective-permute-start | bytes 786440 | tf_op jit(solution)/shard_map/ppermute | solution.py:16
  339.5 4.8 %collective-permute-start.41 = (f32[2,256]{1,0:T(2,128)S(1)}, f32[2,256]{1,0:T(2,128)S(1)}, u32[]{:S(2)}, u32[]{:S(2)}) collective-permute-start(f32[2,256]{1,0:T(2,128)S(1)} %convolution_bitcast_fusion.11), channel_id=1, source_target_pairs={{0,1},{1,0},{2,3},{3,2},{4,5},{5,4},{6,7},{7,6},{8,9},{9,8},{10,11... | collective-permute-start | bytes 6152 | tf_op jit(solution)/shard_map/ppermute | solution.py:16
  344.3 2.5 collective-permute-start.42
  346.8 3.8 %collective-permute-start.43 = (f32[8,256]{1,0:T(8,128)S(1)}, f32[8,256]{1,0:T(8,128)S(1)}, u32[]{:S(2)}, u32[]{:S(2)}) collective-permute-start(f32[8,256]{1,0:T(8,128)S(1)} %maximum_select_fusion.32), channel_id=1, source_target_pairs={{0,4},{4,0},{1,5},{5,1},{2,6},{6,2},{3,7},{7,3},{8,12},{12,8},{9,1... | collective-permute-start | bytes 24584 | tf_op jit(solution)/shard_map/ppermute | solution.py:16
  350.6 6.5 %collective-permute-start.44 = (f32[16,256]{1,0:T(8,128)S(1)}, f32[16,256]{1,0:T(8,128)S(1)}, u32[]{:S(2)}, u32[]{:S(2)}) collective-permute-start(f32[16,256]{1,0:T(8,128)S(1)} %maximum_select_fusion.30), channel_id=1, source_target_pairs={{0,8},{8,0},{1,9},{9,1},{2,10},{10,2},{3,11},{11,3},{4,12},{12,4},... | collective-permute-start | bytes 49160 | tf_op jit(solution)/shard_map/ppermute | solution.py:16
  357.1 3.1 collective-permute-start.45
  360.1 4.7 %collective-permute-start.46 = (f32[64,256]{1,0:T(8,128)S(1)}, f32[64,256]{1,0:T(8,128)S(1)}, u32[]{:S(2)}, u32[]{:S(2)}) collective-permute-start(f32[64,256]{1,0:T(8,128)S(1)} %maximum_select_fusion.23), channel_id=1, source_target_pairs={{0,32},{32,0},{1,33},{33,1},{2,34},{34,2},{3,35},{35,3},{4,36},{36... | collective-permute-start | bytes 196616 | tf_op jit(solution)/shard_map/ppermute | solution.py:16
  364.9 3.9 %collective-permute-start.47 = (f32[128,256]{1,0:T(8,128)S(1)}, f32[128,256]{1,0:T(8,128)S(1)}, u32[]{:S(2)}, u32[]{:S(2)}) collective-permute-start(f32[128,256]{1,0:T(8,128)S(1)} %maximum_select_fusion.19), channel_id=1, source_target_pairs={{0,64},{64,0},{1,65},{65,1},{2,66},{66,2},{3,67},{67,3},{4,68},{68... | collective-permute-start | bytes 393224 | tf_op jit(solution)/shard_map/ppermute | solution.py:16
where the time goes:
time: 378 us; the launch traced here: 371 us
  waiting for transfers between devices  253 us (67%)
  starting transfers between devices  94 us (25%)
  matrix products  21.2 us (6%)
    ppermute x48, waiting for transfers between devices, from_partner(): return lax.ppermute(block, axis, route)  253 us
    ppermute x48, starting transfers between devices, from_partner(): return lax.ppermute(block, axis, route)  94 us
    dot_general x4, matrix products, local(): lax.dot_general(right_rows, solution, (((0,), (0,)), ((), ())), precision...  8.09 us
    dot_general x4, matrix products, local(): jnp.dot(left_rows, gathered, precision=lax.Precision.HIGHEST, preferred_e...  7.92 us
  transfers between devices with their start and end apart: 48, of which 48 were waited for; matrix products, arithmetic and copies ran while one was open for 0% of the time, Pallas kernels for 0%

commit v1 on v0

v1 whole, which is shorter than its diff:
```python
import jax
import jax.numpy as jnp
from jax import lax
from jax.sharding import Mesh, PartitionSpec as P

LEVELS = 4
AXES = ("xh", "xl", "yh", "yl", "z", "c")
SIZES = (2, 2, 2, 2, 8, 2)
Z = 8
HIGHEST = lax.Precision.HIGHEST
F32 = jnp.float32


def split(value):
    high = lax.reduce_precision(value, 8, 7)
    return high.astype(jnp.bfloat16), (value - high).astype(jnp.bfloat16)


def dot(a, b, dims):
    return lax.dot_general(a, b, ((dims[0], dims[1]), ((), ())), preferred_element_type=F32)


def fdot(a, b, dims):
    return lax.dot_general(a, b, ((dims[0], dims[1]), ((), ())), precision=HIGHEST, preferred_element_type=F32)


def exchange(block, axes):
    return lax.all_to_all(block, axes, 0, 0, tiled=True)


def swap_core(block):
    return lax.ppermute(block, "c", [(0, 1), (1, 0)])


def spread(block, axes, count):
    full = jnp.broadcast_to(block[None], (count,) + block.shape)
    return exchange(full, axes)


def scatter_sum(blocks, core):
    n = blocks.shape[0]
    halves = blocks.reshape(n, 2, 128, 256)
    give = jnp.where(core == 0, halves[:, 1], halves[:, 0])
    keep = jnp.where(core == 0, halves[:, 0], halves[:, 1])
    mine = keep + swap_core(give)
    mine = mine.reshape(n, Z, 16, 256).transpose(1, 0, 2, 3)
    return exchange(mine, "z").sum(axis=0)


def gather_rows(block, core):
    n = block.shape[0]
    half = spread(block, "z", Z).transpose(1, 0, 2, 3).reshape(n, 128, 256)
    other = swap_core(half)
    low = jnp.where(core == 0, half, other)
    high = jnp.where(core == 0, other, half)
    return jnp.concatenate([low, high], axis=1)


def local(right_side, leaf_inv, right_basis, left_basis, k1, k2, k3, k4):
    core = lax.axis_index("c")
    rows = jnp.concatenate([k4, k3, k2, k1, jnp.zeros((2, 512), F32)], axis=0)
    by_z = spread(rows, "z", Z)
    part4 = by_z[:, 0:16]
    part3 = spread(by_z[:, 16:24], "yl", 2)
    part2 = spread(by_z[:, 24:28], ("yh", "yl"), 4)
    part1 = spread(by_z[:, 28:30], ("xl", "yh", "yl"), 8)

    def whole(part):
        other = swap_core(part)
        low = jnp.where(core == 0, part, other)
        high = jnp.where(core == 0, other, part)
        return jnp.stack([low, high], axis=-3).reshape(256, 512)

    x0 = dot(leaf_inv, right_side, ((1,), (0,)))
    hi, lo = split(x0)
    hilo = jnp.concatenate([hi, lo], axis=1)

    def project(j):
        both = dot(hilo, right_basis[j - 1], ((0,), (0,)))
        return both[:256] + both[256:]

    def couple(j, k):
        return dot(left_basis[k - 1], right_basis[j - 1], ((0,), (0,)))

    first = jnp.stack([project(4), couple(3, 4)])
    rest = jnp.stack(
        [project(3), project(2), project(1), couple(2, 4), couple(2, 3), couple(1, 4), couple(1, 3), couple(1, 2)]
    )
    first = scatter_sum(first, core)
    rest = scatter_sum(rest, core)
    p4, g34 = first[0], first[1]
    p3, p2, p1 = rest[0], rest[1], rest[2]
    g34 = gather_rows(g34[None], core)[0]
    g2_1 = gather_rows(rest[3:8], core)
    g24, g23, g14, g13, g12 = [g2_1[n] for n in range(5)]

    def mix(part, stack):
        return fdot(stack, whole(part), ((1,), (1,)))

    def times(m, g):
        return fdot(m, g, ((1,), (0,)))

    def sums(t, axes, count):
        got = spread(t, axes, count).reshape(2, count // 2, 16, 256).sum(axis=1)
        return jnp.concatenate([got[0], got[1]], axis=1)

    m4 = mix(part4, sums(p4, "yl", 2))
    t3 = p3 - times(m4, g34)
    m3 = mix(part3, sums(t3, ("yh", "yl"), 4))
    t2 = p2 - times(m4, g24) - times(m3, g23)
    m2 = mix(part2, sums(t2, ("xl", "yh", "yl"), 8))
    t1 = p1 - times(m4, g14) - times(m3, g13) - times(m2, g12)
    m1 = mix(part1, sums(t1, ("xh", "xl", "yh", "yl"), 16))

    def correction(m, level):
        mh, ml = split(m)
        left = left_basis[level - 1]
        return dot(left, mh, ((1,), (1,))) + dot(left, ml, ((1,), (1,)))

    late = gather_rows(jnp.stack([m4, m3, m2]), core)
    out = x0 - correction(late[0], 4) - correction(late[1], 3) - correction(late[2], 2)
    last = gather_rows(m1[None], core)
    return out - correction(last[0], 1)


def solution(mesh):
    fine = Mesh(mesh.devices.reshape(SIZES), AXES)
    row = P(AXES, None)
    level = P(None, AXES, None)
    return jax.shard_map(
        local,
        mesh=fine,
        in_specs=(row, row, level, level, row, row, row, row),
        out_specs=row,
        check_vma=False,
    )
```

time: 378 us -> 243 us (0.64); the launches traced: 371 us -> 241 us
  waiting for transfers between devices: 253 us -> 80.1 us
  local copies, waits for them, and re-layouts: 1.63 us -> 25.1 us
  other arithmetic: 0.89 us -> 18.1 us
  matrix products: 21.2 us -> 29.7 us
  starting transfers between devices: 94 us -> 87.1 us
    ppermute x48 -> x10, waiting for transfers between devices: 253 us -> 0.04 us  [swap_core(): return lax.ppermute(block, 'c', [(0, 1), (1, 0)])]
    all_to_all x0 -> x14, waiting for transfers between devices: none -> 80.1 us  [exchange(): return lax.all_to_all(block, axes, 0, 0, tiled=True)]
    ppermute x48 -> x10, starting transfers between devices: 94 us -> 31.7 us  [swap_core(): return lax.ppermute(block, 'c', [(0, 1), (1, 0)])]
    all_to_all x0 -> x14, starting transfers between devices: none -> 55.4 us  [exchange(): return lax.all_to_all(block, axes, 0, 0, tiled=True)]
    another operation x0 -> x9, other arithmetic: none -> 9.27 us  [the longest x8 9.27 us: whole(): return jnp.stack([low, high], axis=-3).reshape(256, 512)]
    broadcast_in_dim x0 -> x14, local copies, waits for them, and re-layouts: none -> 8.92 us  [the longest x13 8.91 us: spread(): full = jnp.broadcast_to(block[None], (count,) + block.shape)]
    dot_general x13 -> x29, matrix products: 21.2 us -> 29.7 us  [the longest x19 20.9 us: dot(): lax.dot_general(a, b, ((dims[0], dims[1]), ((), ())), preferred_element_t...]
    dot_general x0 -> x4, local copies, waits for them, and re-layouts: none -> 5.83 us  [dot(): lax.dot_general(a, b, ((dims[0], dims[1]), ((), ())), preferred_element_t...]
  transfers between devices with their start and end apart: 48 -> 24, of which waited for: 48 -> 12; matrix products, arithmetic and copies ran while one was open for 0% -> 23% of each run, Pallas kernels for 0% -> 0%
where the time goes in v1:
time: 243 us; the launch traced here: 241 us
  starting transfers between devices  87.1 us (36%)
  waiting for transfers between devices  80.1 us (33%)
  matrix products  29.7 us (12%)
  local copies, waits for them, and re-layouts  25.1 us (10%)
  other arithmetic  18.1 us (7%)
    all_to_all x14, waiting for transfers between devices, exchange(): return lax.all_to_all(block, axes, 0, 0, tiled=True)  80.1 us
    all_to_all x14, starting transfers between devices, exchange(): return lax.all_to_all(block, axes, 0, 0, tiled=True)  55.4 us
    ppermute x10, starting transfers between devices, swap_core(): return lax.ppermute(block, 'c', [(0, 1), (1, 0)])  31.7 us
    dot_general x19, matrix products, dot(): lax.dot_general(a, b, ((dims[0], dims[1]), ((), ())), preferred_element_t...  20.9 us
    another operation x8, other arithmetic, whole(): return jnp.stack([low, high], axis=-3).reshape(256, 512)  9.27 us
    broadcast_in_dim x13, local copies, waits for them, and re-layouts, spread(): full = jnp.broadcast_to(block[None], (count,) + block.shape)  8.91 us
    dot_general x10, matrix products, fdot(): lax.dot_general(a, b, ((dims[0], dims[1]), ((), ())), precision=HIGHEST,...  8.82 us
    dot_general x4, local copies, waits for them, and re-layouts, dot(): lax.dot_general(a, b, ((dims[0], dims[1]), ((), ())), preferred_element_t...  5.83 us
  transfers between devices with their start and end apart: 24, of which 12 were waited for; matrix products, arithmetic and copies ran while one was open for 23% of the time, Pallas kernels for 0%

profile of v1, /device:TPU:1, one launch (start us, length us, event | category | flops | bytes accessed | tf_op | source)
XLA Modules:
  0.0 240.8 jit_solution(12225517701501819441)
XLA Ops:
  0.0 2.6 %slice_bitcast_fusion = (bf16[256,1024]{0,1:T(8,128)(2,1)}, bf16[256,1024]{0,1:T(8,128)(2,1)S(1)}, bf16[256,1024]{0,1:T(8,128)(2,1)}) fusion(bf16[4,1024,256]{2,1,0:T(8,128)(2,1)} %param.11), kind=kLoop, calls=%fused_computation.88 | loop fusion | bytes 3145728 | tf_op jit(solution)/shard_map/dot_general | solution.py:20
  2.8 2.9 %reduce-precision_convert_fusion = (bf16[1024,256]{0,1:T(8,128)(2,1)S(1)}, bf16[1024,256]{0,1:T(8,128)(2,1)S(1)}, f32[1024,256]{0,1:T(8,128)}) fusion(bf16[1024,1024]{1,0:T(8,128)(2,1)S(1)} %copy-done, bf16[1024,256]{1,0:T(8,128)(2,1)} %param.8), kind=kOutput, calls=%fused_computation.9 | convolution fusion | flops 537919488 | bytes 4718592 | tf_op jit(solution)/shard_map/dot_general | solution.py:20
  7.8 3.2 %collective-permute-start = (f32[2,128,256]{2,1,0:T(8,128)}, f32[2,128,256]{2,1,0:T(8,128)S(1)}, u32[]{:S(2)}, u32[]{:S(2)}) collective-permute-start(f32[2,128,256]{2,1,0:T(8,128)} %select_bitcast_fusion.9), channel_id=1, source_target_pairs={{0,1},{1,0},{2,3},{3,2},{4,5},{5,4},{6,7},{7,6},{8,9},{9,8},{10,11... | collective-permute-start | bytes 786440 | tf_op jit(solution)/shard_map/ppermute | solution.py:32
  11.0 1.8 fusion.35
  16.1 2.0 copy.82
  18.1 2.0 fusion.12
  20.9 6.5 %all-to-all-start = ((f32[8,2,16,256]{3,2,1,0:T(8,128)}), f32[8,2,16,256]{3,2,1,0:T(8,128)S(1)}, u32[]{:S(2)}, u32[]{:S(2)}) async-start(f32[8,2,16,256]{3,2,1,0:T(8,128)} %bitcast.281), calls=%async_computation | async-start | bytes 524288 | tf_op jit(solution)/shard_map/all_to_all | solution.py:28
  27.4 2.3 fusion.11
  29.7 2.1 fusion.10
  31.8 7.3 %all-to-all-done = f32[8,2,16,256]{3,2,1,0:T(8,128)S(1)} async-done(((f32[8,2,16,256]{3,2,1,0:T(8,128)}), f32[8,2,16,256]{3,2,1,0:T(8,128)S(1)}, u32[]{:S(2)}, u32[]{:S(2)}) %all-to-all-start) | async-done | bytes 262176 | tf_op jit(solution)/shard_map/all_to_all | solution.py:28
  39.8 3.3 %all-to-all-start.1 = ((f32[2,16,256]{2,1,0:T(8,128)}), f32[2,16,256]{2,1,0:T(8,128)S(1)}, u32[]{:S(2)}, u32[]{:S(2)}) async-start(f32[2,16,256]{2,1,0:T(8,128)} %broadcast_in_dim.31), calls=%async_computation.1 | async-start | bytes 65536 | tf_op jit(solution)/shard_map/all_to_all | solution.py:28
  43.0 2.2 fusion.9
  45.2 1.0 copy.83
  46.3 0.9 broadcast_in_dim.33
  47.2 3.5 %all-to-all-start.2 = ((f32[8,32,512]{2,1,0:T(8,128)}), f32[8,32,512]{2,1,0:T(8,128)S(1)}, u32[]{:S(2)}, u32[]{:S(2)}) async-start(f32[8,32,512]{2,1,0:T(8,128)} %broadcast_in_dim.33), calls=%async_computation.2 | async-start | bytes 1048576 | tf_op jit(solution)/shard_map/all_to_all | solution.py:28
  50.7 2.2 fusion.8
  52.9 2.6 %select_bitcast_fusion = f32[8,128,256]{2,1,0:T(8,128)} fusion(f32[8,2,128,256]{3,2,1,0:T(8,128)} %fusion.8, pred[]{:T(512)S(6)} %eq.2), kind=kLoop, calls=%fused_computation.45 | loop fusion | flops 262144 | bytes 3145729 | tf_op jit(solution)/shard_map/jit(_where)/select_n | solution.py:43
  55.5 1.8 collective-permute-start.2
  57.3 9.3 %all-to-all-done.2 = f32[8,32,512]{2,1,0:T(8,128)S(1)} async-done(((f32[8,32,512]{2,1,0:T(8,128)}), f32[8,32,512]{2,1,0:T(8,128)S(1)}, u32[]{:S(2)}, u32[]{:S(2)}) %all-to-all-start.2) | async-done | bytes 524320 | tf_op jit(solution)/shard_map/all_to_all | solution.py:28
  67.3 3.4 %all-to-all-start.4 = ((f32[8,1,16,256]{3,2,1,0:T(8,128)}), f32[8,1,16,256]{3,2,1,0:T(8,128)S(1)}, u32[]{:S(2)}, u32[]{:S(2)}) async-start(f32[8,1,16,256]{3,2,1,0:T(8,128)} %broadcast_in_dim.35), calls=%async_computation.4 | async-start | bytes 262144 | tf_op jit(solution)/shard_map/all_to_all | solution.py:28
  70.7 7.9 %all-to-all-done.4 = f32[8,1,16,256]{3,2,1,0:T(8,128)S(1)} async-done(((f32[8,1,16,256]{3,2,1,0:T(8,128)}), f32[8,1,16,256]{3,2,1,0:T(8,128)S(1)}, u32[]{:S(2)}, u32[]{:S(2)}) %all-to-all-start.4) | async-done | bytes 131104 | tf_op jit(solution)/shard_map/all_to_all | solution.py:28
  79.3 3.4 %all-to-all-start.6 = ((f32[2,8,8,512]{3,2,1,0:T(8,128)}), f32[2,8,8,512]{3,2,1,0:T(8,128)S(1)}, u32[]{:S(2)}, u32[]{:S(2)}) async-start(f32[2,8,8,512]{3,2,1,0:T(8,128)} %broadcast_in_dim.37), calls=%async_computation.6 | async-start | bytes 524288 | tf_op jit(solution)/shard_map/all_to_all | solution.py:28
  82.8 4.6 %all-to-all-done.6 = f32[2,8,8,512]{3,2,1,0:T(8,128)S(1)} async-done(((f32[2,8,8,512]{3,2,1,0:T(8,128)}), f32[2,8,8,512]{3,2,1,0:T(8,128)S(1)}, u32[]{:S(2)}, u32[]{:S(2)}) %all-to-all-start.6) | async-done | bytes 262176 | tf_op jit(solution)/shard_map/all_to_all | solution.py:28
  88.2 4.2 %all-to-all-start.9 = ((f32[4,8,4,512]{3,2,1,0:T(4,128)}), f32[4,8,4,512]{3,2,1,0:T(4,128)S(1)}, u32[]{:S(2)}, u32[]{:S(2)}) async-start(f32[4,8,4,512]{3,2,1,0:T(4,128)} %broadcast_in_dim.40), calls=%async_computation.9 | async-start | bytes 524288 | tf_op jit(solution)/shard_map/all_to_all | solution.py:28
  92.4 5.5 %all-to-all-done.9 = f32[4,8,4,512]{3,2,1,0:T(4,128)S(1)} async-done(((f32[4,8,4,512]{3,2,1,0:T(4,128)}), f32[4,8,4,512]{3,2,1,0:T(4,128)S(1)}, u32[]{:S(2)}, u32[]{:S(2)}) %all-to-all-start.9) | async-done | bytes 262176 | tf_op jit(solution)/shard_map/all_to_all | solution.py:28
  98.7 4.0 %all-to-all-start.12 = ((f32[8,8,2,512]{3,2,1,0:T(2,128)}), f32[8,8,2,512]{3,2,1,0:T(2,128)}, u32[]{:S(2)}, u32[]{:S(2)}) async-start(f32[8,8,2,512]{3,2,1,0:T(2,128)} %broadcast_in_dim.43), calls=%async_computation.12 | async-start | bytes 524288 | tf_op jit(solution)/shard_map/all_to_all | solution.py:28
  102.8 2.1 fusion.15
  104.9 1.1 copy.99
  106.0 2.9 %all-to-all-done.12 = f32[8,8,2,512]{3,2,1,0:T(2,128)} async-done(((f32[8,8,2,512]{3,2,1,0:T(2,128)}), f32[8,8,2,512]{3,2,1,0:T(2,128)}, u32[]{:S(2)}, u32[]{:S(2)}) %all-to-all-start.12) | async-done | bytes 262176 | tf_op jit(solution)/shard_map/all_to_all | solution.py:28
  108.9 3.6 %all-to-all-start.3 = ((f32[8,8,16,256]{3,2,1,0:T(8,128)}), f32[8,8,16,256]{3,2,1,0:T(8,128)S(1)}, u32[]{:S(2)}, u32[]{:S(2)}) async-start(f32[8,8,16,256]{3,2,1,0:T(8,128)} %bitcast.280), calls=%async_computation.3 | async-start | bytes 2097152 | tf_op jit(solution)/shard_map/all_to_all | solution.py:28
  112.4 1.0 slice.210
  113.4 6.7 %collective-permute-start.1 = (f32[8,16,512]{2,1,0:T(8,128)S(1)}, f32[8,16,512]{2,1,0:T(8,128)S(1)}, u32[]{:S(2)}, u32[]{:S(2)}) collective-permute-start(f32[8,16,512]{2,1,0:T(8,128)S(1)} %slice.210), channel_id=1, source_target_pairs={{0,1},{1,0},{2,3},{3,2},{4,5},{5,4},{6,7},{7,6},{8,9},{9,8},{10,11... | collective-permute-start | bytes 786440 | tf_op jit(solution)/shard_map/ppermute | solution.py:32
  120.2 1.3 slice_bitcast_fusion.14
  123.2 1.8 select_bitcast_fusion.8
  125.0 11.8 %all-to-all-done.3 = f32[8,8,16,256]{3,2,1,0:T(8,128)S(1)} async-done(((f32[8,8,16,256]{3,2,1,0:T(8,128)}), f32[8,8,16,256]{3,2,1,0:T(8,128)S(1)}, u32[]{:S(2)}, u32[]{:S(2)}) %all-to-all-start.3) | async-done | bytes 1048608 | tf_op jit(solution)/shard_map/all_to_all | solution.py:28
  136.9 0.9 broadcast_in_dim.38
  137.8 3.5 %all-to-all-start.7 = ((f32[8,5,16,256]{3,2,1,0:T(8,128)}), f32[8,5,16,256]{3,2,1,0:T(8,128)S(1)}, u32[]{:S(2)}, u32[]{:S(2)}) async-start(f32[8,5,16,256]{3,2,1,0:T(8,128)} %broadcast_in_dim.38), calls=%async_computation.7 | async-start | bytes 1310720 | tf_op jit(solution)/shard_map/all_to_all | solution.py:28
  141.4 1.1 pad_maximum_fusion.1
  142.5 1.3 fusion.99
  143.8 1.0 select_bitcast_fusion.6
  145.7 1.9 select_bitcast_fusion.4
  147.7 8.6 %all-to-all-done.7 = f32[8,5,16,256]{3,2,1,0:T(8,128)S(1)} async-done(((f32[8,5,16,256]{3,2,1,0:T(8,128)}), f32[8,5,16,256]{3,2,1,0:T(8,128)S(1)}, u32[]{:S(2)}, u32[]{:S(2)}) %all-to-all-start.7) | async-done | bytes 655392 | tf_op jit(solution)/shard_map/all_to_all | solution.py:28
  157.0 3.9 %all-to-all-start.5 = ((f32[4,16,256]{2,1,0:T(8,128)}), f32[4,16,256]{2,1,0:T(8,128)}, u32[]{:S(2)}, u32[]{:S(2)}) async-start(f32[4,16,256]{2,1,0:T(8,128)} %broadcast_in_dim.36), calls=%async_computation.5 | async-start | bytes 131072 | tf_op jit(solution)/shard_map/all_to_all | solution.py:28
  161.0 6.5 %collective-permute-start.5 = (f32[5,128,256]{2,1,0:T(8,128)S(1)}, f32[5,128,256]{2,1,0:T(8,128)}, u32[]{:S(2)}, u32[]{:S(2)}) collective-permute-start(f32[5,128,256]{2,1,0:T(8,128)S(1)} %bitcast.283), channel_id=1, source_target_pairs={{0,1},{1,0},{2,3},{3,2},{4,5},{5,4},{6,7},{7,6},{8,9},{9,8},{10,11... | collective-permute-start | bytes 1966088 | tf_op jit(solution)/shard_map/ppermute | solution.py:32
  167.4 1.2 pad_maximum_fusion.3
  168.6 1.0 reshape.167
  170.4 1.6 fusion.103
  172.0 1.4 broadcast_select_fusion
  175.4 4.5 %all-to-all-start.8 = ((f32[8,16,256]{2,1,0:T(8,128)}), f32[8,16,256]{2,1,0:T(8,128)S(1)}, u32[]{:S(2)}, u32[]{:S(2)}) async-start(f32[8,16,256]{2,1,0:T(8,128)} %broadcast_in_dim.39), calls=%async_computation.8 | async-start | bytes 262144 | tf_op jit(solution)/shard_map/all_to_all | solution.py:28
  180.0 1.6 convolution_subtract_fusion.1
  181.6 3.9 %all-to-all-done.8 = f32[8,16,256]{2,1,0:T(8,128)S(1)} async-done(((f32[8,16,256]{2,1,0:T(8,128)}), f32[8,16,256]{2,1,0:T(8,128)S(1)}, u32[]{:S(2)}, u32[]{:S(2)}) %all-to-all-start.8) | async-done | bytes 131104 | tf_op jit(solution)/shard_map/all_to_all | solution.py:28
  185.4 1.6 fusion.107
  187.0 0.9 convolution_subtract_fusion
  188.7 4.8 %all-to-all-start.11 = ((f32[16,16,256]{2,1,0:T(8,128)}), f32[16,16,256]{2,1,0:T(8,128)S(1)}, u32[]{:S(2)}, u32[]{:S(2)}) async-start(f32[16,16,256]{2,1,0:T(8,128)} %broadcast_in_dim.42), calls=%async_computation.11 | async-start | bytes 524288 | tf_op jit(solution)/shard_map/all_to_all | solution.py:28
  193.5 1.2 select_bitcast_fusion.2
  195.4 5.4 %all-to-all-done.11 = f32[16,16,256]{2,1,0:T(8,128)S(1)} async-done(((f32[16,16,256]{2,1,0:T(8,128)}), f32[16,16,256]{2,1,0:T(8,128)S(1)}, u32[]{:S(2)}, u32[]{:S(2)}) %all-to-all-start.11) | async-done | bytes 262176 | tf_op jit(solution)/shard_map/all_to_all | solution.py:28
  202.0 3.4 %all-to-all-start.13 = ((f32[8,1,16,256]{3,2,1,0:T(8,128)}), f32[8,1,16,256]{3,2,1,0:T(8,128)S(1)}, u32[]{:S(2)}, u32[]{:S(2)}) async-start(f32[8,1,16,256]{3,2,1,0:T(8,128)} %broadcast_in_dim.44), calls=%async_computation.13 | async-start | bytes 262144 | tf_op jit(solution)/shard_map/all_to_all | solution.py:28
  205.4 7.8 %all-to-all-done.13 = f32[8,1,16,256]{3,2,1,0:T(8,128)S(1)} async-done(((f32[8,1,16,256]{3,2,1,0:T(8,128)}), f32[8,1,16,256]{3,2,1,0:T(8,128)S(1)}, u32[]{:S(2)}, u32[]{:S(2)}) %all-to-all-start.13) | async-done | bytes 131104 | tf_op jit(solution)/shard_map/all_to_all | solution.py:28
  214.0 3.5 %all-to-all-start.10 = ((f32[8,3,16,256]{3,2,1,0:T(8,128)}), f32[8,3,16,256]{3,2,1,0:T(8,128)S(1)}, u32[]{:S(2)}, u32[]{:S(2)}) async-start(f32[8,3,16,256]{3,2,1,0:T(8,128)} %broadcast_in_dim.41), calls=%async_computation.10 | async-start | bytes 786432 | tf_op jit(solution)/shard_map/all_to_all | solution.py:28
  217.5 5.7 %collective-permute-start.9 = (f32[1,128,256]{2,1,0:T(8,128)S(1)}, f32[1,128,256]{2,1,0:T(8,128)S(1)}, u32[]{:S(2)}, u32[]{:S(2)}) collective-permute-start(f32[1,128,256]{2,1,0:T(8,128)S(1)} %bitcast.298), channel_id=1, source_target_pairs={{0,1},{1,0},{2,3},{3,2},{4,5},{5,4},{6,7},{7,6},{8,9},{9,8},{10,11... | collective-permute-start | bytes 393224 | tf_op jit(solution)/shard_map/ppermute | solution.py:32
  223.2 5.0 %all-to-all-done.10 = f32[8,3,16,256]{3,2,1,0:T(8,128)S(1)} async-done(((f32[8,3,16,256]{3,2,1,0:T(8,128)}), f32[8,3,16,256]{3,2,1,0:T(8,128)S(1)}, u32[]{:S(2)}, u32[]{:S(2)}) %all-to-all-start.10) | async-done | bytes 393248 | tf_op jit(solution)/shard_map/all_to_all | solution.py:28
  228.2 6.8 %collective-permute-start.7 = (f32[3,128,256]{2,1,0:T(8,128)S(1)}, f32[3,128,256]{2,1,0:T(8,128)S(1)}, u32[]{:S(2)}, u32[]{:S(2)}) collective-permute-start(f32[3,128,256]{2,1,0:T(8,128)S(1)} %bitcast.291), channel_id=1, source_target_pairs={{0,1},{1,0},{2,3},{3,2},{4,5},{5,4},{6,7},{7,6},{8,9},{9,8},{10,11... | collective-permute-start | bytes 1179656 | tf_op jit(solution)/shard_map/ppermute | solution.py:32
  235.0 1.4 fusion.17
  239.5 1.3 copy.94
  (123 shorter events, 22.7 us)
Async XLA Ops:
  0.0 2.8 %copy-start = (bf16[1024,1024]{1,0:T(8,128)(2,1)S(1)}, bf16[1024,1024]{1,0:T(8,128)(2,1)}, u32[]{:S(2)}) copy-start(bf16[1024,1024]{1,0:T(8,128)(2,1)} %param.9) | copy-start | bytes 6291460
  2.8 2.9 %copy-start.16 = (bf16[4,1024,256]{2,1,0:T(8,128)(2,1)S(1)}, bf16[4,1024,256]{2,1,0:T(8,128)(2,1)}, u32[]{:S(2)}) copy-start(bf16[4,1024,256]{2,1,0:T(8,128)(2,1)} %param.10) | copy-start | bytes 6291460
  5.7 0.8 copy-start.8
  5.7 1.0 copy-start.10
  7.1 5.8 %copy-start.9 = (bf16[1024,256]{0,1:T(8,128)(2,1)S(1)}, bf16[1024,256]{0,1:T(8,128)(2,1)}, u32[]{:S(2)}) copy-start(bf16[1024,256]{0,1:T(8,128)(2,1)} %copy-done.8) | copy-start | bytes 1572868
  7.1 5.8 %copy-start.11 = (bf16[1024,256]{0,1:T(8,128)(2,1)S(1)}, bf16[1024,256]{0,1:T(8,128)(2,1)}, u32[]{:S(2)}) copy-start(bf16[1024,256]{0,1:T(8,128)(2,1)} %copy-done.10) | copy-start | bytes 1572868
  7.1 5.8 %copy-start.17 = (bf16[4,1024,256]{2,1,0:T(8,128)(2,1)S(1)}, bf16[4,1024,256]{2,1,0:T(8,128)(2,1)}, u32[]{:S(2)}) copy-start(bf16[4,1024,256]{2,1,0:T(8,128)(2,1)} %param.10) | copy-start | bytes 6291460
  7.8 12.3 %collective-permute-start = (f32[2,128,256]{2,1,0:T(8,128)}, f32[2,128,256]{2,1,0:T(8,128)S(1)}, u32[]{:S(2)}, u32[]{:S(2)}) collective-permute-start(f32[2,128,256]{2,1,0:T(8,128)} %select_bitcast_fusion.9), channel_id=1, source_target_pairs={{0,1},{1,0},{2,3},{3,2},{4,5},{5,4},{6,7},{7,6},{8,9},{9,8},{10,11... | collective-permute-start | bytes 786440 | tf_op jit(solution)/shard_map/ppermute | solution.py:32
  20.9 18.2 %all-to-all-start = ((f32[8,2,16,256]{3,2,1,0:T(8,128)}), f32[8,2,16,256]{3,2,1,0:T(8,128)S(1)}, u32[]{:S(2)}, u32[]{:S(2)}) async-start(f32[8,2,16,256]{3,2,1,0:T(8,128)} %bitcast.281), calls=%async_computation | async-start | bytes 524288 | tf_op jit(solution)/shard_map/all_to_all | solution.py:28
  27.4 17.8 %copy-start.5 = (bf16[256,1024]{0,1:T(8,128)(2,1)S(1)}, bf16[256,1024]{0,1:T(8,128)(2,1)}, u32[]{:S(2)}) copy-start(bf16[256,1024]{0,1:T(8,128)(2,1)} %get-tuple-element.5) | copy-start | bytes 1572868
  29.7 16.5 %copy-start.19 = (f32[16,512]{1,0:T(8,128)S(1)}, f32[16,512]{1,0:T(8,128)}, u32[]{:S(2)}) copy-start(f32[16,512]{1,0:T(8,128)} %param.15) | copy-start | bytes 98308
  29.7 16.5 %copy-start.20 = (f32[8,512]{1,0:T(8,128)S(1)}, f32[8,512]{1,0:T(8,128)}, u32[]{:S(2)}) copy-start(f32[8,512]{1,0:T(8,128)} %param.14) | copy-start | bytes 49156
  29.7 16.5 %copy-start.21 = (f32[4,512]{1,0:T(4,128)S(1)}, f32[4,512]{1,0:T(4,128)}, u32[]{:S(2)}) copy-start(f32[4,512]{1,0:T(4,128)} %param.13) | copy-start | bytes 24580
  29.7 16.6 %copy-start.22 = (f32[2,512]{1,0:T(2,128)S(1)}, f32[2,512]{1,0:T(2,128)}, u32[]{:S(2)}) copy-start(f32[2,512]{1,0:T(2,128)} %param.12) | copy-start | bytes 12292
  39.8 6.5 %all-to-all-start.1 = ((f32[2,16,256]{2,1,0:T(8,128)}), f32[2,16,256]{2,1,0:T(8,128)S(1)}, u32[]{:S(2)}, u32[]{:S(2)}) async-start(f32[2,16,256]{2,1,0:T(8,128)} %broadcast_in_dim.31), calls=%async_computation.1 | async-start | bytes 65536 | tf_op jit(solution)/shard_map/all_to_all | solution.py:28
  46.3 0.9 copy-start.18
  47.2 19.4 %all-to-all-start.2 = ((f32[8,32,512]{2,1,0:T(8,128)}), f32[8,32,512]{2,1,0:T(8,128)S(1)}, u32[]{:S(2)}, u32[]{:S(2)}) async-start(f32[8,32,512]{2,1,0:T(8,128)} %broadcast_in_dim.33), calls=%async_computation.2 | async-start | bytes 1048576 | tf_op jit(solution)/shard_map/all_to_all | solution.py:28
  55.5 47.3 %collective-permute-start.2 = (f32[8,128,256]{2,1,0:T(8,128)}, f32[8,128,256]{2,1,0:T(8,128)}, u32[]{:S(2)}, u32[]{:S(2)}) collective-permute-start(f32[8,128,256]{2,1,0:T(8,128)} %select_bitcast_fusion), channel_id=1, source_target_pairs={{0,1},{1,0},{2,3},{3,2},{4,5},{5,4},{6,7},{7,6},{8,9},{9,8},{10,11... | collective-permute-start | bytes 3145736 | tf_op jit(solution)/shard_map/ppermute | solution.py:32
  66.6 38.3 %copy-start.3 = (f32[8,32,512]{2,1,0:T(8,128)}, f32[8,32,512]{2,1,0:T(8,128)S(1)}, u32[]{:S(2)}) copy-start(f32[8,32,512]{2,1,0:T(8,128)S(1)} %all-to-all-done.2) | copy-start | bytes 1572868
  67.3 11.3 %all-to-all-start.4 = ((f32[8,1,16,256]{3,2,1,0:T(8,128)}), f32[8,1,16,256]{3,2,1,0:T(8,128)S(1)}, u32[]{:S(2)}, u32[]{:S(2)}) async-start(f32[8,1,16,256]{3,2,1,0:T(8,128)} %broadcast_in_dim.35), calls=%async_computation.4 | async-start | bytes 262144 | tf_op jit(solution)/shard_map/all_to_all | solution.py:28
  79.3 8.1 %all-to-all-start.6 = ((f32[2,8,8,512]{3,2,1,0:T(8,128)}), f32[2,8,8,512]{3,2,1,0:T(8,128)S(1)}, u32[]{:S(2)}, u32[]{:S(2)}) async-start(f32[2,8,8,512]{3,2,1,0:T(8,128)} %broadcast_in_dim.37), calls=%async_computation.6 | async-start | bytes 524288 | tf_op jit(solution)/shard_map/all_to_all | solution.py:28
  88.2 9.7 %all-to-all-start.9 = ((f32[4,8,4,512]{3,2,1,0:T(4,128)}), f32[4,8,4,512]{3,2,1,0:T(4,128)S(1)}, u32[]{:S(2)}, u32[]{:S(2)}) async-start(f32[4,8,4,512]{3,2,1,0:T(4,128)} %broadcast_in_dim.40), calls=%async_computation.9 | async-start | bytes 524288 | tf_op jit(solution)/shard_map/all_to_all | solution.py:28
  97.9 6.9 %copy-start.6 = (f32[4,8,4,512]{3,2,1,0:T(4,128)}, f32[4,8,4,512]{3,2,1,0:T(4,128)S(1)}, u32[]{:S(2)}) copy-start(f32[4,8,4,512]{3,2,1,0:T(4,128)S(1)} %all-to-all-done.9) | copy-start | bytes 786436
  98.7 10.1 %all-to-all-start.12 = ((f32[8,8,2,512]{3,2,1,0:T(2,128)}), f32[8,8,2,512]{3,2,1,0:T(2,128)}, u32[]{:S(2)}, u32[]{:S(2)}) async-start(f32[8,8,2,512]{3,2,1,0:T(2,128)} %broadcast_in_dim.43), calls=%async_computation.12 | async-start | bytes 524288 | tf_op jit(solution)/shard_map/all_to_all | solution.py:28
  108.9 27.9 %all-to-all-start.3 = ((f32[8,8,16,256]{3,2,1,0:T(8,128)}), f32[8,8,16,256]{3,2,1,0:T(8,128)S(1)}, u32[]{:S(2)}, u32[]{:S(2)}) async-start(f32[8,8,16,256]{3,2,1,0:T(8,128)} %bitcast.280), calls=%async_computation.3 | async-start | bytes 2097152 | tf_op jit(solution)/shard_map/all_to_all | solution.py:28
  113.4 9.8 %collective-permute-start.1 = (f32[8,16,512]{2,1,0:T(8,128)S(1)}, f32[8,16,512]{2,1,0:T(8,128)S(1)}, u32[]{:S(2)}, u32[]{:S(2)}) collective-permute-start(f32[8,16,512]{2,1,0:T(8,128)S(1)} %slice.210), channel_id=1, source_target_pairs={{0,1},{1,0},{2,3},{3,2},{4,5},{5,4},{6,7},{7,6},{8,9},{9,8},{10,11... | collective-permute-start | bytes 786440 | tf_op jit(solution)/shard_map/ppermute | solution.py:32
  120.1 1.9 collective-permute-start.3
  121.5 22.3 %collective-permute-start.4 = (f32[2,8,8,512]{3,2,1,0:T(8,128)S(1)}, f32[2,8,8,512]{3,2,1,0:T(8,128)}, u32[]{:S(2)}, u32[]{:S(2)}) collective-permute-start(f32[2,8,8,512]{3,2,1,0:T(8,128)S(1)} %all-to-all-done.6), channel_id=1, source_target_pairs={{0,1},{1,0},{2,3},{3,2},{4,5},{5,4},{6,7},{7,6},{8,9},{9,8},{10,11... | collective-permute-start | bytes 786440 | tf_op jit(solution)/shard_map/ppermute | solution.py:32
  122.7 23.0 %collective-permute-start.6 = (f32[4,8,4,512]{3,2,1,0:T(4,128)}, f32[4,8,4,512]{3,2,1,0:T(4,128)}, u32[]{:S(2)}, u32[]{:S(2)}) collective-permute-start(f32[4,8,4,512]{3,2,1,0:T(4,128)} %copy-done.6), channel_id=1, source_target_pairs={{0,1},{1,0},{2,3},{3,2},{4,5},{5,4},{6,7},{7,6},{8,9},{9,8},{10,11... | collective-permute-start | bytes 786440 | tf_op jit(solution)/shard_map/ppermute | solution.py:32
  122.8 70.7 %collective-permute-start.8 = (f32[8,8,2,512]{3,2,1,0:T(2,128)}, f32[8,8,2,512]{3,2,1,0:T(2,128)}, u32[]{:S(2)}, u32[]{:S(2)}) collective-permute-start(f32[8,8,2,512]{3,2,1,0:T(2,128)} %all-to-all-done.12), channel_id=1, source_target_pairs={{0,1},{1,0},{2,3},{3,2},{4,5},{5,4},{6,7},{7,6},{8,9},{9,8},{10,11... | collective-permute-start | bytes 786440 | tf_op jit(solution)/shard_map/ppermute | solution.py:32
  137.8 18.5 %all-to-all-start.7 = ((f32[8,5,16,256]{3,2,1,0:T(8,128)}), f32[8,5,16,256]{3,2,1,0:T(8,128)S(1)}, u32[]{:S(2)}, u32[]{:S(2)}) async-start(f32[8,5,16,256]{3,2,1,0:T(8,128)} %broadcast_in_dim.38), calls=%async_computation.7 | async-start | bytes 1310720 | tf_op jit(solution)/shard_map/all_to_all | solution.py:28
  141.4 4.3 %copy-start.7 = (f32[4,8,4,512]{3,2,1,0:T(4,128)S(1)}, f32[4,8,4,512]{3,2,1,0:T(4,128)}, u32[]{:S(2)}) copy-start(f32[4,8,4,512]{3,2,1,0:T(4,128)} %copy-done.6) | copy-start | bytes 786436
  142.5 5.0 %copy-start.12 = (f32[1,128,256]{2,1,0:T(8,128)S(1)}, f32[1,128,256]{2,1,0:T(8,128)}, u32[]{:S(2)}) copy-start(f32[1,128,256]{2,1,0:T(8,128)} %get-tuple-element.24) | copy-start | bytes 393220
  142.5 5.0 %copy-start.13 = (f32[1,128,256]{2,1,0:T(8,128)S(1)}, f32[1,128,256]{2,1,0:T(8,128)}, u32[]{:S(2)}) copy-start(f32[1,128,256]{2,1,0:T(8,128)} %get-tuple-element.25) | copy-start | bytes 393220
  157.0 12.6 %all-to-all-start.5 = ((f32[4,16,256]{2,1,0:T(8,128)}), f32[4,16,256]{2,1,0:T(8,128)}, u32[]{:S(2)}, u32[]{:S(2)}) async-start(f32[4,16,256]{2,1,0:T(8,128)} %broadcast_in_dim.36), calls=%async_computation.5 | async-start | bytes 131072 | tf_op jit(solution)/shard_map/all_to_all | solution.py:28
  160.9 11.1 %copy-start.4 = (f32[8,5,16,256]{3,2,0,1:T(8,128)}, f32[8,5,16,256]{3,2,0,1:T(8,128)S(1)}, u32[]{:S(2)}) copy-start(f32[8,5,16,256]{3,2,0,1:T(8,128)S(1)} %copy.90) | copy-start | bytes 1966084
  161.0 11.1 %collective-permute-start.5 = (f32[5,128,256]{2,1,0:T(8,128)S(1)}, f32[5,128,256]{2,1,0:T(8,128)}, u32[]{:S(2)}, u32[]{:S(2)}) collective-permute-start(f32[5,128,256]{2,1,0:T(8,128)S(1)} %bitcast.283), channel_id=1, source_target_pairs={{0,1},{1,0},{2,3},{3,2},{4,5},{5,4},{6,7},{7,6},{8,9},{9,8},{10,11... | collective-permute-start | bytes 1966088 | tf_op jit(solution)/shard_map/ppermute | solution.py:32
  172.0 2.5 %copy-start.14 = (f32[16,256]{1,0:T(8,128)}, f32[16,256]{1,0:T(8,128)S(1)}, u32[]{:S(2)}) copy-start(f32[16,256]{1,0:T(8,128)S(1)} %fusion.103) | copy-start | bytes 49156
  175.4 10.0 %all-to-all-start.8 = ((f32[8,16,256]{2,1,0:T(8,128)}), f32[8,16,256]{2,1,0:T(8,128)S(1)}, u32[]{:S(2)}, u32[]{:S(2)}) async-start(f32[8,16,256]{2,1,0:T(8,128)} %broadcast_in_dim.39), calls=%async_computation.8 | async-start | bytes 262144 | tf_op jit(solution)/shard_map/all_to_all | solution.py:28
  188.7 12.1 %all-to-all-start.11 = ((f32[16,16,256]{2,1,0:T(8,128)}), f32[16,16,256]{2,1,0:T(8,128)S(1)}, u32[]{:S(2)}, u32[]{:S(2)}) async-start(f32[16,16,256]{2,1,0:T(8,128)} %broadcast_in_dim.42), calls=%async_computation.11 | async-start | bytes 524288 | tf_op jit(solution)/shard_map/all_to_all | solution.py:28
  193.5 11.9 %copy-start.15 = (f32[16,256]{1,0:T(8,128)S(1)}, f32[16,256]{1,0:T(8,128)}, u32[]{:S(2)}) copy-start(f32[16,256]{1,0:T(8,128)} %copy-done.14) | copy-start | bytes 49156
  202.0 11.2 %all-to-all-start.13 = ((f32[8,1,16,256]{3,2,1,0:T(8,128)}), f32[8,1,16,256]{3,2,1,0:T(8,128)S(1)}, u32[]{:S(2)}, u32[]{:S(2)}) async-start(f32[8,1,16,256]{3,2,1,0:T(8,128)} %broadcast_in_dim.44), calls=%async_computation.13 | async-start | bytes 262144 | tf_op jit(solution)/shard_map/all_to_all | solution.py:28
  214.0 14.1 %all-to-all-start.10 = ((f32[8,3,16,256]{3,2,1,0:T(8,128)}), f32[8,3,16,256]{3,2,1,0:T(8,128)S(1)}, u32[]{:S(2)}, u32[]{:S(2)}) async-start(f32[8,3,16,256]{3,2,1,0:T(8,128)} %broadcast_in_dim.41), calls=%async_computation.10 | async-start | bytes 786432 | tf_op jit(solution)/shard_map/all_to_all | solution.py:28
  217.5 17.5 %collective-permute-start.9 = (f32[1,128,256]{2,1,0:T(8,128)S(1)}, f32[1,128,256]{2,1,0:T(8,128)S(1)}, u32[]{:S(2)}, u32[]{:S(2)}) collective-permute-start(f32[1,128,256]{2,1,0:T(8,128)S(1)} %bitcast.298), channel_id=1, source_target_pairs={{0,1},{1,0},{2,3},{3,2},{4,5},{5,4},{6,7},{7,6},{8,9},{9,8},{10,11... | collective-permute-start | bytes 393224 | tf_op jit(solution)/shard_map/ppermute | solution.py:32
  228.2 8.3 %copy-start.1 = (bf16[4,1024,256]{2,1,0:T(8,128)(2,1)S(1)}, bf16[4,1024,256]{2,1,0:T(8,128)(2,1)}, u32[]{:S(2)}) copy-start(bf16[4,1024,256]{2,1,0:T(8,128)(2,1)} %param.11) | copy-start | bytes 6291460
  228.2 8.3 %collective-permute-start.7 = (f32[3,128,256]{2,1,0:T(8,128)S(1)}, f32[3,128,256]{2,1,0:T(8,128)S(1)}, u32[]{:S(2)}, u32[]{:S(2)}) collective-permute-start(f32[3,128,256]{2,1,0:T(8,128)S(1)} %bitcast.291), channel_id=1, source_target_pairs={{0,1},{1,0},{2,3},{3,2},{4,5},{5,4},{6,7},{7,6},{8,9},{9,8},{10,11... | collective-permute-start | bytes 1179656 | tf_op jit(solution)/shard_map/ppermute | solution.py:32
  236.8 1.2 copy-start.2
